TPU v7x, 512 devices: a whole 4x8x8 slice. The times are simulated.
512 devices in a mesh: snode: 64 (over z, y), rows: 8 (over x, core).
Axes of the slice: x: 4, y: 8, z: 8, core: 2. Of those that a mesh axis runs over, the one named last changes fastest.
Arguments:
- anc_store: bfloat16 [8192, 8192], P('snode'), may hold values from -9 to 9
- patterns: int32 [64, 8], replicated, may hold values from 0 to 63, all different within a row
- tile_counts: int32 [64], replicated, may hold values from 1 to 8, 448 in all
- tile_owner: int32 [64], replicated, may hold values from 0 to 63, as said below
- l_offdiag: bfloat16 [65536, 512], P(('snode', 'rows')), may hold values from -0.25 to 0.25
- diag_inverse: bfloat16 [32768, 512], P(('snode', 'rows')), may hold values from -1 to 2, as said below
Outputs:
- sigma_offdiag: bfloat16 [65536, 512], P(('snode', 'rows'))
- sigma_diag: float32 [32768, 512], P(('snode', 'rows'))
Inputs may be any that keep to these rules, and one draw needn't show every extreme that they name: `patterns`: each supernode's row names 8 different ancestor tiles. Slots before tile_counts[s] of a supernode's pattern are live, the rest padding; some supernode has all 8 slots live. `tile_owner`: a permutation of the ancestor tiles. `diag_inverse`: each supernode's block of 512 rows is lower triangular with diagonal entries between 1 and 2.
All inputs are finite; a program needn't handle non-finite values.
Results may differ from a plain program's by a relative error of at most 0.014.
Values may be sent and summed in bfloat16 or wider, within the bound.
A program may use at most 64 MiB of HBM per device.

v0:
```python
import jax
import jax.numpy as jnp
from jax import lax
from jax.sharding import PartitionSpec as P


def row_block(matrix, index):
    return lax.dynamic_index_in_dim(matrix, index, 0, keepdims=False)


def per_device(anc_store, patterns, tile_counts, tile_owner, l_offdiag, diag_inverse):
    tile_rows = anc_store.shape[0]
    pool_size = tile_owner.shape[0]
    group_count = patterns.shape[0]
    pattern_len = patterns.shape[1]
    group_id = lax.axis_index("snode")
    part_id = lax.axis_index("rows")
    local_tiles = l_offdiag.shape[0] // tile_rows
    band_rows = diag_inverse.shape[0]
    band_start = part_id * band_rows
    live_mask = jnp.arange(pattern_len, dtype=jnp.int32)[None, :] < tile_counts[:, None]
    own_live = lax.dynamic_slice_in_dim(
        row_block(live_mask, group_id), part_id * local_tiles, local_tiles
    )
    keep_rows = jnp.repeat(own_live, tile_rows)
    masked_l = jnp.where(keep_rows[:, None], l_offdiag, jnp.zeros_like(l_offdiag))
    piece = lax.all_gather(diag_inverse, "rows", axis=0, tiled=True)
    u_total = jnp.dot(masked_l, piece, preferred_element_type=jnp.float32)
    own_cols = lax.dynamic_slice_in_dim(piece, band_start, band_rows, 1)
    d_total = lax.dot_general(
        own_cols, piece, (((0,), (0,)), ((), ())), preferred_element_type=jnp.float32
    )
    u_total, base_diag = (u_total, d_total)
    u_factor = u_total.astype(jnp.bfloat16)
    owned_tile = jnp.sum(
        jnp.arange(pool_size, dtype=jnp.int32) * (tile_owner == group_id).astype(jnp.int32)
    )
    send_flag = jnp.any((patterns == owned_tile) & live_mask, axis=1)
    own_pattern = row_block(patterns, group_id)
    sources = jnp.take(tile_owner, own_pattern, axis=0)
    col_tiles = lax.dynamic_slice_in_dim(patterns, part_id * local_tiles, local_tiles, 1)
    stored_blocks = anc_store.reshape(tile_rows, pool_size, tile_rows)
    picked = jnp.take(stored_blocks, col_tiles, axis=1)
    picked = jnp.transpose(picked, (1, 0, 2, 3)).reshape(
        group_count, tile_rows, local_tiles * tile_rows
    )
    outgoing = jnp.where(send_flag[:, None, None], picked, jnp.zeros_like(picked))
    incoming = lax.all_to_all(outgoing, "snode", split_axis=0, concat_axis=0, tiled=True)
    arranged = jnp.take(incoming, sources, axis=0).reshape(
        pattern_len * tile_rows, local_tiles * tile_rows
    )
    own_rows = lax.all_to_all(arranged, "rows", split_axis=0, concat_axis=1, tiled=True)
    y_block = jnp.dot(
        own_rows,
        lax.all_gather(u_factor, "rows", axis=0, tiled=True),
        preferred_element_type=jnp.float32,
    )
    offdiag = (-y_block).astype(jnp.bfloat16)
    partial_diag = lax.dot_general(
        u_factor, offdiag, (((0,), (0,)), ((), ())), preferred_element_type=jnp.float32
    )
    whole_update = lax.psum(partial_diag.astype(jnp.bfloat16), "rows").astype(jnp.float32)
    reduced = lax.dynamic_slice_in_dim(whole_update, band_start, band_rows, 0)
    return (offdiag, base_diag - reduced)


def solution(mesh):
    in_specs = (
        P("snode", None),
        P(),
        P(),
        P(),
        P(("snode", "rows"), None),
        P(("snode", "rows"), None),
    )
    out_specs = (P(("snode", "rows"), None), P(("snode", "rows"), None))
    return jax.shard_map(
        per_device, mesh=mesh, in_specs=in_specs, out_specs=out_specs, check_vma=False
    )
```

profile of v0, /device:TPU:8, one launch (start us, length us, event | category | flops | bytes accessed | tf_op | source)
XLA Modules:
  0.0 179.3 jit_solution(5158815995826037886)
XLA Ops:
  7.2 0.7 and_bitcast_fusion
  7.9 3.2 %copy.8 = bf16[128,8192]{0,1:T(8,128)(2,1)S(1)} copy(bf16[128,8192]{1,0:T(8,128)(2,1)} %param.6) | data formatting | bytes 4194304 | tf_op args[0]
  11.1 2.9 %copy.9 = bf16[128,64,128]{2,0,1:T(8,128)(2,1)} copy(bf16[128,64,128]{0,2,1:T(8,128)(2,1)S(1)} %bitcast.37) | data formatting | bytes 4194304 | tf_op jit(solution)/shard_map/reshape | solution.py:42
  14.0 0.0 copy-start
  14.0 0.0 copy-start.5
  14.0 0.0 copy-start.6
  14.0 2.6 %gather_fusion.1 = bf16[64,128,128]{2,1,0:T(8,128)(2,1)S(1)} fusion(bf16[128,64,128]{2,0,1:T(8,128)(2,1)} %copy.9, s32[1024]{0:T(1024)S(1)} %pad_clamp_fusion.1), kind=kCustom, calls=%fused_computation.1 | custom fusion | bytes 4194560 | tf_op jit(solution)/shard_map/jit(_take)/gather | solution.py:43
  16.6 0.0 copy-done
  16.6 0.6 fusion.6
  17.2 0.0 copy-done.5
  17.2 0.0 copy-done.6
  17.3 0.7 iota_compare_fusion
  17.9 1.7 bitcast_select_fusion
  19.6 0.0 copy-start.4
  19.6 0.0 copy-start.3
  19.6 16.7 %all-to-all-start = ((bf16[64,128,128]{2,1,0:T(8,128)(2,1)}), bf16[64,128,128]{2,1,0:T(8,128)(2,1)S(1)}, u32[]{:S(2)}, u32[]{:S(2)}) async-start(bf16[64,128,128]{2,1,0:T(8,128)(2,1)} %bitcast_select_fusion), calls=%async_computation | async-start | bytes 4194304 | tf_op jit(solution)/shard_map/all_to_all | solution.py:48
  36.3 0.0 all-gather.2.cloned.1.call-start
  36.4 0.6 dynamic_slice.22
  37.0 0.0 copy-done.4
  37.0 13.4 %all_gather.6 = bf16[512,512]{1,0:T(8,128)(2,1)S(1)} all-gather(bf16[64,512]{1,0:T(8,128)(2,1)S(1)} %copy-done.4), channel_id=1, replica_groups=mesh['snode'=64,'rows'=8] {'rows'}, dimensions={0}, use_global_device_ids=true | all-gather | bytes 589824 | tf_op jit(solution)/shard_map/all_gather | solution.py:27
  50.4 0.0 copy-done.3
  50.4 1.5 convolution_convert_fusion.1
  52.0 0.0 copy-start.1
  52.0 0.0 all-gather.2.cloned.1.call-update
  52.0 0.0 all-reduce.2.cloned.1.call-start
  52.0 0.2 dynamic-slice_reduce_fusion
  52.2 0.6 gather_fusion
  52.9 36.3 %all-to-all-done = bf16[64,128,128]{2,1,0:T(8,128)(2,1)S(1)} async-done(((bf16[64,128,128]{2,1,0:T(8,128)(2,1)}), bf16[64,128,128]{2,1,0:T(8,128)(2,1)S(1)}, u32[]{:S(2)}, u32[]{:S(2)}) %all-to-all-start) | async-done | bytes 2097184 | tf_op jit(solution)/shard_map/all_to_all | solution.py:48
  89.2 0.6 gather_fusion.2
  89.8 0.1 broadcast_select_fusion
  89.9 11.6 %all_to_all.21 = bf16[8,128,128]{2,1,0:T(8,128)(2,1)S(1)} all-to-all(bf16[8,128,128]{2,1,0:T(8,128)(2,1)S(1)} %broadcast_select_fusion), channel_id=1, replica_groups=mesh['snode'=64,'rows'=8] {'rows'}, dimensions={0} | all-to-all | bytes 524288 | tf_op jit(solution)/shard_map/all_to_all | solution.py:52
  101.6 0.2 copy.10
  101.8 0.0 all-gather.2.cloned.1.call-done
  101.8 1.6 fusion
  103.3 0.0 copy-done.1
  103.4 0.0 copy-start.2
  103.4 1.1 convolution_convert_fusion
  104.5 0.0 all-reduce.2.cloned.1.call-update
  104.5 66.2 %all-reduce.2.cloned.1.call-done = bf16[512,512]{1,0:T(8,128)(2,1)} async-done(((bf16[512,512]{1,0:T(8,128)(2,1)}), bf16[512,512]{1,0:T(8,128)(2,1)}) %all-reduce.2.cloned.1.call-update) | async-done | bytes 524304 | tf_op jit(solution)/shard_map/psum | solution.py:62
  170.7 1.8 %convolution_subtract_fusion = f32[64,512]{1,0:T(8,128)} fusion(bf16[512,512]{1,0:T(8,128)(2,1)S(1)} %all_gather.6, s32[]{:T(128)S(6)} %select_n.116, bf16[512,512]{1,0:T(8,128)(2,1)} %all-reduce.2.cloned.1.call-done), kind=kOutput, calls=%fused_computation.9 | convolution fusion | flops 33619968 | bytes 852992 | tf_op jit(solution)/shard_map/dot_general | solution.py:30
  172.5 0.0 copy-done.2
  (6 shorter events, 0.0 us)
Async XLA Ops:
  14.0 2.6 %copy-start = (s32[64]{0:T(128)S(1)}, s32[64]{0:T(128)}, u32[]{:S(2)}) copy-start(s32[64]{0:T(128)} %param.9) | copy-start | bytes 772
  14.0 3.2 %copy-start.5 = (s32[64,8]{0,1:T(8,128)S(1)}, s32[64,8]{0,1:T(8,128)}, u32[]{:S(2)}) copy-start(s32[64,8]{0,1:T(8,128)} %param.7) | copy-start | bytes 6148
  14.0 3.2 %copy-start.6 = (s32[64]{0:T(128)S(1)}, s32[64]{0:T(128)}, u32[]{:S(2)}) copy-start(s32[64]{0:T(128)} %param.8) | copy-start | bytes 772
  19.6 17.4 %copy-start.4 = (bf16[64,512]{1,0:T(8,128)(2,1)S(1)}, bf16[64,512]{1,0:T(8,128)(2,1)}, u32[]{:S(2)}) copy-start(bf16[64,512]{1,0:T(8,128)(2,1)} %param.11) | copy-start | bytes 196612
  19.6 30.8 %copy-start.3 = (bf16[128,512]{1,0:T(8,128)(2,1)S(1)}, bf16[128,512]{1,0:T(8,128)(2,1)}, u32[]{:S(2)}) copy-start(bf16[128,512]{1,0:T(8,128)(2,1)} %param.10) | copy-start | bytes 393220
  19.6 69.6 %all-to-all-start = ((bf16[64,128,128]{2,1,0:T(8,128)(2,1)}), bf16[64,128,128]{2,1,0:T(8,128)(2,1)S(1)}, u32[]{:S(2)}, u32[]{:S(2)}) async-start(bf16[64,128,128]{2,1,0:T(8,128)(2,1)} %bitcast_select_fusion), calls=%async_computation | async-start | bytes 4194304 | tf_op jit(solution)/shard_map/all_to_all | solution.py:48
  36.3 65.5 %all-gather.2.cloned.1.call-start = ((), (), s32[]{:S(2)}) async-start(), calls=%async_computation.2 | async-start | bytes 1179648 | tf_op jit(solution)/shard_map/all_gather | solution.py:55
  52.0 51.4 %copy-start.1 = (bf16[128,512]{1,0:T(8,128)(2,1)S(1)}, bf16[128,512]{1,0:T(8,128)(2,1)}, u32[]{:S(2)}) copy-start(bf16[128,512]{1,0:T(8,128)(2,1)} %convolution_convert_fusion.1) | copy-start | bytes 393220
  52.0 118.7 %all-reduce.2.cloned.1.call-start = ((), (), s32[]{:S(2)}) async-start(), calls=%async_computation.3 | async-start | bytes 1048576 | tf_op jit(solution)/shard_map/psum | solution.py:62
  103.4 69.1 %copy-start.2 = (bf16[128,512]{1,0:T(8,128)(2,1)}, bf16[128,512]{1,0:T(8,128)(2,1)S(1)}, u32[]{:S(2)}) copy-start(bf16[128,512]{1,0:T(8,128)(2,1)S(1)} %fusion) | copy-start | bytes 393220
Sparse Core Ops, SparseCore 0:
  52.1 28.7 all-gather.1
  104.6 65.9 all-reduce.1
where the time goes:
time: 180 us; the launch traced here: 179 us
  waiting for transfers between devices  103 us (57%)
  blocking collectives  25.1 us (14%)
  starting transfers between devices  16.8 us (9%)
  between operations  14.2 us (8%)
  local copies, waits for them, and re-layouts  10.9 us (6%)
  matrix products  6 us (3%)
  other arithmetic  3.82 us (2%)
    psum x1, waiting for transfers between devices, per_device(): lax.psum(partial_diag.astype(jnp.bfloat16), 'rows').astype(jnp.float32)  66.2 us
    all_to_all x1, waiting for transfers between devices, per_device(): lax.all_to_all(outgoing, 'snode', split_axis=0, concat_axis=0, tiled=True)  36.3 us
    all_to_all x1, starting transfers between devices, per_device(): lax.all_to_all(outgoing, 'snode', split_axis=0, concat_axis=0, tiled=True)  16.7 us
    all_gather x1, blocking collectives, per_device(): piece = lax.all_gather(diag_inverse, 'rows', axis=0, tiled=True)  13.4 us
    all_to_all x1, blocking collectives, per_device(): lax.all_to_all(arranged, 'rows', split_axis=0, concat_axis=1, tiled=True)  11.6 us
  transfers between devices with their start and end apart: 3, of which 2 were waited for; matrix products, arithmetic and copies ran while one was open for 2% of the time, Pallas kernels for 0%

commit v1 on v0

--- a/solution.py
+++ b/solution.py
@@ -1,7 +1,15 @@
+import functools
 import jax
 import jax.numpy as jnp
 from jax import lax
 from jax.sharding import PartitionSpec as P
+
+
+def meshes_meet(field, named_axis):
+    return lax.all_gather(field, axis_name=named_axis).sum(axis=0)
+
+
+post_row_up = functools.partial(meshes_meet, named_axis="rows")
 
 
 def row_block(matrix, index):
@@ -59,7 +67,7 @@
     partial_diag = lax.dot_general(
         u_factor, offdiag, (((0,), (0,)), ((), ())), preferred_element_type=jnp.float32
     )
-    whole_update = lax.psum(partial_diag.astype(jnp.bfloat16), "rows").astype(jnp.float32)
+    whole_update = post_row_up(partial_diag.astype(jnp.bfloat16)).astype(jnp.float32)
     reduced = lax.dynamic_slice_in_dim(whole_update, band_start, band_rows, 0)
     return (offdiag, base_diag - reduced)
 

time: 180 us -> 149 us (0.83)
  the two profiles are of different devices: /device:TPU:8 before, /device:TPU:1 now
where the time goes in v1:
time: 149 us
  waiting for transfers between devices  65.6 us (44%)
  blocking collectives  28.9 us (19%)
  starting transfers between devices  17.4 us (12%)
  between operations  14.2 us (10%)
  local copies, waits for them, and re-layouts  10.9 us (7%)
  other arithmetic  6.87 us (5%)
  matrix products  5.19 us (3%)
    all_gather x1, waiting for transfers between devices, meshes_meet(): return lax.all_gather(field, axis_name=named_axis).sum(axis=0)  33.7 us
    all_to_all x1, waiting for transfers between devices, per_device(): lax.all_to_all(outgoing, 'snode', split_axis=0, concat_axis=0, tiled=True)  31.9 us
    all_to_all x1, starting transfers between devices, per_device(): lax.all_to_all(outgoing, 'snode', split_axis=0, concat_axis=0, tiled=True)  17.3 us
    all_to_all x1, blocking collectives, per_device(): lax.all_to_all(arranged, 'rows', split_axis=0, concat_axis=1, tiled=True)  14.6 us
    all_gather x1, blocking collectives, per_device(): piece = lax.all_gather(diag_inverse, 'rows', axis=0, tiled=True)  14.2 us
    unnamed x15, local copies, waits for them, and re-layouts  3.25 us
    reduce_sum x1, other arithmetic, meshes_meet(): return lax.all_gather(field, axis_name=named_axis).sum(axis=0)  3.06 us
  transfers between devices with their start and end apart: 3, of which 2 were waited for; matrix products, arithmetic and copies ran while one was open for 3% of the time, Pallas kernels for 0%

profile of v1, /device:TPU:1, one launch (start us, length us, event | category | flops | bytes accessed | tf_op | source)
XLA Modules:
  0.0 149.0 jit_solution(2967641892347117014)
XLA Ops:
  7.2 0.7 and_bitcast_fusion
  7.9 3.2 %copy.8 = bf16[128,8192]{0,1:T(8,128)(2,1)S(1)} copy(bf16[128,8192]{1,0:T(8,128)(2,1)} %param.6) | data formatting | bytes 4194304 | tf_op args[0]
  11.1 2.9 %copy.9 = bf16[128,64,128]{2,0,1:T(8,128)(2,1)} copy(bf16[128,64,128]{0,2,1:T(8,128)(2,1)S(1)} %bitcast.38) | data formatting | bytes 4194304 | tf_op jit(solution)/shard_map/reshape | solution.py:50
  14.0 0.0 copy-start
  14.0 0.0 copy-start.5
  14.0 0.0 copy-start.6
  14.0 2.6 %gather_fusion.1 = bf16[64,128,128]{2,1,0:T(8,128)(2,1)S(1)} fusion(bf16[128,64,128]{2,0,1:T(8,128)(2,1)} %copy.9, s32[1024]{0:T(1024)S(1)} %pad_clamp_fusion.1), kind=kCustom, calls=%fused_computation.1 | custom fusion | bytes 4194560 | tf_op jit(solution)/shard_map/jit(_take)/gather | solution.py:51
  16.6 0.0 copy-done
  16.6 0.6 fusion.6
  17.2 0.0 copy-done.5
  17.2 0.0 copy-done.6
  17.3 0.7 iota_compare_fusion
  17.9 1.7 %bitcast_select_fusion = bf16[64,128,128]{2,1,0:T(8,128)(2,1)} fusion(bf16[64,128,128]{2,1,0:T(8,128)(2,1)S(1)} %gather_fusion.1, pred[64]{0:T(512)(128)(4,1)S(1)} %get-tuple-element.2, pred[64]{0:T(512)(128)(4,1)S(1)} %get-tuple-element.5), kind=kLoop, calls=%fused_computation.3 | loop fusion | flops 2097152 | bytes 4194432 | tf_op jit(solution)/shard_map/jit(_where)/select_n | solution.py:55
  19.6 0.0 copy-start.4
  19.6 0.0 copy-start.3
  19.6 17.3 %all-to-all-start = ((bf16[64,128,128]{2,1,0:T(8,128)(2,1)}), bf16[64,128,128]{2,1,0:T(8,128)(2,1)S(1)}, u32[]{:S(2)}, u32[]{:S(2)}) async-start(bf16[64,128,128]{2,1,0:T(8,128)(2,1)} %bitcast_select_fusion), calls=%async_computation | async-start | bytes 4194304 | tf_op jit(solution)/shard_map/all_to_all | solution.py:56
  36.9 0.0 all-gather.4.cloned.1.call-start
  36.9 0.6 dynamic_slice.22
  37.5 0.0 copy-done.4
  37.5 14.2 %all_gather.12 = bf16[512,512]{1,0:T(8,128)(2,1)S(1)} all-gather(bf16[64,512]{1,0:T(8,128)(2,1)S(1)} %copy-done.4), channel_id=1, replica_groups=mesh['snode'=64,'rows'=8] {'rows'}, dimensions={0}, use_global_device_ids=true | all-gather | bytes 589824 | tf_op jit(solution)/shard_map/all_gather | solution.py:35
  51.8 0.0 copy-done.3
  51.8 1.5 %convolution_convert_fusion.1 = bf16[128,512]{1,0:T(8,128)(2,1)} fusion(bf16[512,512]{1,0:T(8,128)(2,1)S(1)} %all_gather.12, bf16[128,512]{1,0:T(8,128)(2,1)S(1)} %copy-done.3, pred[]{:T(512)} %bitcast.12), kind=kOutput, calls=%fused_computation.7 | convolution fusion | flops 67239936 | bytes 786433 | tf_op jit(solution)/shard_map/dot_general | solution.py:36
  53.3 0.0 copy-start.1
  53.3 0.0 all-gather.4.cloned.1.call-update
  53.3 0.0 all-gather.6.cloned.1.call-start
  53.4 0.2 dynamic-slice_reduce_fusion
  53.6 0.6 gather_fusion
  54.3 31.9 %all-to-all-done = bf16[64,128,128]{2,1,0:T(8,128)(2,1)S(1)} async-done(((bf16[64,128,128]{2,1,0:T(8,128)(2,1)}), bf16[64,128,128]{2,1,0:T(8,128)(2,1)S(1)}, u32[]{:S(2)}, u32[]{:S(2)}) %all-to-all-start) | async-done | bytes 2097184 | tf_op jit(solution)/shard_map/all_to_all | solution.py:56
  86.2 0.6 gather_fusion.2
  86.8 0.1 broadcast_select_fusion
  86.9 14.6 %all_to_all.21 = bf16[8,128,128]{2,1,0:T(8,128)(2,1)S(1)} all-to-all(bf16[8,128,128]{2,1,0:T(8,128)(2,1)S(1)} %broadcast_select_fusion), channel_id=1, replica_groups=mesh['snode'=64,'rows'=8] {'rows'}, dimensions={0} | all-to-all | bytes 524288 | tf_op jit(solution)/shard_map/all_to_all | solution.py:60
  101.5 0.2 copy.10
  101.7 0.0 all-gather.4.cloned.1.call-done
  101.7 1.6 %fusion = bf16[128,512]{1,0:T(8,128)(2,1)S(1)} fusion(bf16[128,1024]{0,1:T(8,128)(2,1)S(1)} %bitcast.41, bf16[1024,512]{1,0:T(8,128)(2,1)} %all-gather.4.cloned.1.call-done), kind=kOutput, calls=%fused_computation.8 | convolution fusion | flops 134348800 | bytes 1441792 | tf_op jit(solution)/shard_map/dot_general | solution.py:61
  103.3 0.0 copy-done.1
  103.3 0.0 copy-start.2
  103.3 1.1 convolution_convert_fusion
  104.4 0.0 all-gather.6.cloned.1.call-update
  104.5 33.7 %all-gather.6.cloned.1.call-done = bf16[4096,512]{1,0:T(8,128)(2,1)} async-done(((bf16[512,512]{1,0:T(8,128)(2,1)}), bf16[4096,512]{1,0:T(8,128)(2,1)}) %all-gather.6.cloned.1.call-update) | async-done | bytes 4194320 | tf_op jit(solution)/shard_map/all_gather | solution.py:9
  138.1 3.1 %reduce_sum.22 = bf16[512,512]{1,0:T(8,128)(2,1)S(1)} reduce(bf16[8,512,512]{2,1,0:T(8,128)(2,1)} %bitcast.39, bf16[]{:T(256)} %constant.81.clone.1), dimensions={0}, to_apply=%region_2.3 | reduce | flops 1835008 | bytes 4718594 | tf_op jit(solution)/shard_map/reduce_sum | solution.py:9
  141.2 0.0 copy-done.2
  141.2 1.0 convolution_subtract_fusion
  (6 shorter events, 0.0 us)
Async XLA Ops:
  14.0 2.6 %copy-start = (s32[64]{0:T(128)S(1)}, s32[64]{0:T(128)}, u32[]{:S(2)}) copy-start(s32[64]{0:T(128)} %param.9) | copy-start | bytes 772
  14.0 3.2 %copy-start.5 = (s32[64,8]{0,1:T(8,128)S(1)}, s32[64,8]{0,1:T(8,128)}, u32[]{:S(2)}) copy-start(s32[64,8]{0,1:T(8,128)} %param.7) | copy-start | bytes 6148
  14.0 3.2 %copy-start.6 = (s32[64]{0:T(128)S(1)}, s32[64]{0:T(128)}, u32[]{:S(2)}) copy-start(s32[64]{0:T(128)} %param.8) | copy-start | bytes 772
  19.6 17.9 %copy-start.4 = (bf16[64,512]{1,0:T(8,128)(2,1)S(1)}, bf16[64,512]{1,0:T(8,128)(2,1)}, u32[]{:S(2)}) copy-start(bf16[64,512]{1,0:T(8,128)(2,1)} %param.11) | copy-start | bytes 196612
  19.6 32.2 %copy-start.3 = (bf16[128,512]{1,0:T(8,128)(2,1)S(1)}, bf16[128,512]{1,0:T(8,128)(2,1)}, u32[]{:S(2)}) copy-start(bf16[128,512]{1,0:T(8,128)(2,1)} %param.10) | copy-start | bytes 393220
  19.6 66.6 %all-to-all-start = ((bf16[64,128,128]{2,1,0:T(8,128)(2,1)}), bf16[64,128,128]{2,1,0:T(8,128)(2,1)S(1)}, u32[]{:S(2)}, u32[]{:S(2)}) async-start(bf16[64,128,128]{2,1,0:T(8,128)(2,1)} %bitcast_select_fusion), calls=%async_computation | async-start | bytes 4194304 | tf_op jit(solution)/shard_map/all_to_all | solution.py:56
  36.9 64.8 %all-gather.4.cloned.1.call-start = ((), (), s32[]{:S(2)}) async-start(), calls=%async_computation.2 | async-start | bytes 1179648 | tf_op jit(solution)/shard_map/all_gather | solution.py:63
  53.3 50.0 %copy-start.1 = (bf16[128,512]{1,0:T(8,128)(2,1)S(1)}, bf16[128,512]{1,0:T(8,128)(2,1)}, u32[]{:S(2)}) copy-start(bf16[128,512]{1,0:T(8,128)(2,1)} %convolution_convert_fusion.1) | copy-start | bytes 393220
  53.3 84.8 %all-gather.6.cloned.1.call-start = ((), (), s32[]{:S(2)}) async-start(), calls=%async_computation.3 | async-start | bytes 4718592 | tf_op jit(solution)/shard_map/all_gather | solution.py:9
  103.3 37.9 %copy-start.2 = (bf16[128,512]{1,0:T(8,128)(2,1)}, bf16[128,512]{1,0:T(8,128)(2,1)S(1)}, u32[]{:S(2)}) copy-start(bf16[128,512]{1,0:T(8,128)(2,1)S(1)} %fusion) | copy-start | bytes 393220
Sparse Core Ops, SparseCore 0:
  53.4 28.7 all-gather.3
  104.6 33.5 all-gather.5
